TPU v7x, 512 devices: a whole 4x8x8 slice. The times are simulated.
512 devices in a mesh: grp: 16 (over y, core), mdl: 32 (over x, z).
Axes of the slice: x: 4, y: 8, z: 8, core: 2. Of those that a mesh axis runs over, the one named last changes fastest.
Arguments:
- row_states: bfloat16 [6144, 1024], P('grp', 'mdl'), may hold values from -6 to 6
- ffn_gain: bfloat16 [1024], replicated, may hold values from 0.25 to 1.75
- ffn_in: bfloat16 [1024, 32768], P('grp', 'mdl'), may hold values from -0.1875 to 0.1875
- ffn_out: bfloat16 [32768, 1024], P('mdl', 'grp'), may hold values from -0.0625 to 0.0625
- final_gain: bfloat16 [1024], replicated, may hold values from 0.25 to 1.75
- kv_weight: bfloat16 [2, 1024, 16384], P(None, None, 'mdl'), may hold values from -0.1875 to 0.1875
- queries: bfloat16 [4096, 16384], P('grp', 'mdl'), may hold values from -36 to 36
- attn_out: bfloat16 [16384, 1024], P('mdl'), may hold values from -0.75 to 0.75
- row_question: int32 [6144], replicated, may hold values from 0 to 15, as said below
Outputs:
- cross_out: bfloat16 [4096, 1024], P(('grp', 'mdl'))
Inputs may be any that keep to these rules, and one draw needn't show every extreme that they name: `row_question`: within each block of 384 rows (one row group) the rows are sorted by question; in every block each question owns a multiple of 8 rows, at least 8 and at most 72, and one question, drawn from the seed, owns exactly 72 rows of every block.
All inputs are finite; a program needn't handle non-finite values.
Results may differ from a plain program's by a relative error of at most 0.029.
Values may be sent and summed in bfloat16 or wider, within the bound.
No kernel may reach another device: no remote copies, remote signals or barrier semaphores. Data moves between devices by JAX's collectives and lax.ppermute only.
A program may use at most 64 MiB of HBM per device.

v0:
```python
import jax
import jax.numpy as jnp
from jax import lax
from jax.sharding import PartitionSpec as P

HEAD_DIM = 128


def rms_normalize(states, gain):
    wide = states.astype(jnp.float32)
    factor = lax.rsqrt(jnp.mean(wide * wide, axis=-1, keepdims=True) + 1e-06)
    return (wide * factor * gain.astype(jnp.float32)).astype(jnp.bfloat16)


def bucket_plan(row_question, rows_local, groups, my_group):
    capacity = 3 * rows_local // groups
    owners = row_question.reshape(groups, rows_local)
    owner_table = (owners[:, :, None] == jnp.arange(groups, dtype=jnp.int32)[None, None, :]).astype(
        jnp.int32
    )
    counts = jnp.sum(owner_table, axis=1)
    starts = jnp.cumsum(counts, axis=1) - counts
    slot_index = jnp.arange(capacity, dtype=jnp.int32)
    sent_counts = lax.dynamic_index_in_dim(counts, my_group, 0, keepdims=False)
    sent_starts = lax.dynamic_index_in_dim(starts, my_group, 0, keepdims=False)
    send_valid = slot_index[None, :] < sent_counts[:, None]
    send_rows = jnp.minimum(sent_starts[:, None] + slot_index[None, :], rows_local - 1)
    got_counts = lax.dynamic_index_in_dim(counts, my_group, 1, keepdims=False)
    got_valid = (slot_index[None, :] < got_counts[:, None]).reshape(-1)
    return (capacity, send_rows, send_valid, got_valid)


def pack_slots(source, send_rows, send_valid):
    picked = jnp.take(source, send_rows.reshape(-1), axis=0)
    picked = picked.reshape(send_rows.shape[0], send_rows.shape[1], source.shape[1])
    picked = jnp.where(send_valid[:, :, None], picked, jnp.zeros((), source.dtype))
    return picked.reshape(send_rows.shape[0], -1)


def local(
    row_states, ffn_gain, ffn_in, ffn_out, final_gain, kv_weight, queries, attn_out, row_question
):
    groups = lax.axis_size("grp")
    my_group = lax.axis_index("grp")
    rows_local = row_states.shape[0]
    full_rows = lax.all_gather(row_states, "mdl", axis=1, tiled=True)
    normed = rms_normalize(full_rows, ffn_gain)
    pre_active = jnp.dot(
        normed,
        lax.all_gather(ffn_in, "grp", axis=0, tiled=True),
        preferred_element_type=jnp.float32,
    )
    hidden = jnp.maximum(pre_active, 0.0).astype(jnp.bfloat16)
    ffn_terms = jnp.dot(
        hidden,
        lax.all_gather(ffn_out, "grp", axis=1, tiled=True),
        preferred_element_type=jnp.float32,
    )
    ffn_sum = lax.psum_scatter(ffn_terms, "mdl", scatter_dimension=1, tiled=True)
    enc_state = (row_states.astype(jnp.float32) + ffn_sum).astype(jnp.bfloat16)
    capacity, send_rows, send_valid, got_valid = bucket_plan(
        row_question, rows_local, groups, my_group
    )
    head_cols = kv_weight.shape[2]
    outgoing = pack_slots(enc_state, send_rows, send_valid)
    arrived = lax.all_to_all(outgoing, "grp", split_axis=0, concat_axis=0, tiled=True)
    slot_rows = lax.all_gather(arrived.reshape(groups * capacity, -1), "mdl", axis=1, tiled=True)
    encoded = rms_normalize(slot_rows, final_gain)
    projected = jnp.einsum(
        "rd,kdc->krc", encoded, kv_weight, preferred_element_type=jnp.float32
    ).astype(jnp.bfloat16)
    key_rows = projected[0]
    value_rows = projected[1]
    targets = queries.shape[0]
    heads_local = head_cols // HEAD_DIM
    query_heads = queries.reshape(targets, heads_local, HEAD_DIM)
    key_heads = key_rows.reshape(-1, heads_local, HEAD_DIM)
    value_heads = value_rows.reshape(-1, heads_local, HEAD_DIM)
    scores = jnp.einsum("thd,rhd->htr", query_heads, key_heads, preferred_element_type=jnp.float32)
    slot_mask = got_valid[None, None, :]
    scores = jnp.where(slot_mask, scores, -1e30)
    top_score = jnp.max(scores, axis=-1, keepdims=True)
    raised = jnp.where(slot_mask, jnp.exp(scores - top_score), 0.0)
    probabilities = (raised / jnp.sum(raised, axis=-1, keepdims=True)).astype(jnp.bfloat16)
    attended = jnp.einsum(
        "htr,rhd->thd", probabilities, value_heads, preferred_element_type=jnp.float32
    )
    attended = attended.astype(jnp.bfloat16).reshape(targets, head_cols)
    return lax.psum_scatter(
        jnp.dot(attended, attn_out, preferred_element_type=jnp.float32).astype(jnp.bfloat16),
        "mdl",
        scatter_dimension=0,
        tiled=True,
    )


def solution(mesh):
    in_specs = (
        P("grp", "mdl"),
        P(),
        P("grp", "mdl"),
        P("mdl", "grp"),
        P(),
        P(None, None, "mdl"),
        P("grp", "mdl"),
        P("mdl", None),
        P(),
    )
    out_specs = P(("grp", "mdl"), None)
    return jax.shard_map(local, mesh=mesh, in_specs=in_specs, out_specs=out_specs, check_vma=False)
```

profile of v0, /device:TPU:8, one launch (start us, length us, event | category | flops | bytes accessed | tf_op | source)
XLA Modules:
  0.0 669.9 jit_solution(2616351746955564816)
XLA Ops:
  6.5 0.7 all-gather.4.cloned.1.call-update
  7.3 0.7 all-gather.6.cloned.1.call-update
  8.1 0.7 convert_element_type.51
  8.7 56.0 %all_gather.12 = bf16[384,1024]{0,1:T(8,128)(2,1)S(1)} all-gather(bf16[384,32]{0,1:T(8,128)(2,1)} %param.9), channel_id=1, replica_groups=mesh['grp'=16,'mdl'=32] {'mdl'}, dimensions={1}, use_global_device_ids=true | all-gather | bytes 811008 | tf_op jit(solution)/shard_map/all_gather | solution.py:46
  64.7 0.2 fusion.14
  65.0 33.6 %all-gather.6.cloned.1.call-done = bf16[1024,1024]{0,1:T(8,128)(2,1)} async-done(((bf16[1024,64]{0,1:T(8,128)(2,1)}), bf16[1024,1024]{0,1:T(8,128)(2,1)}) %all-gather.6.cloned.1.call-update) | async-done | bytes 2097168 | tf_op jit(solution)/shard_map/all_gather | solution.py:56
  98.5 5.6 fusion.22
  104.2 0.4 convert_reduce_fusion
  104.6 0.2 reduce_window_sum.11
  105.0 0.2 broadcast_in_dim.60
  105.2 0.2 broadcast_in_dim.61
  105.5 0.2 broadcast_in_dim.62
  105.7 0.2 broadcast_in_dim.63
  106.0 222.1 %reduce-scatter.3.cloned.1.call-done = f32[384,32]{0,1:T(8,128)} async-done(((f32[384,1024]{0,1:T(8,128)}), f32[384,32]{0,1:T(8,128)}) %reduce-scatter.3.cloned.1.call-update) | async-done | bytes 49168 | tf_op jit(solution)/shard_map/reduce_scatter | solution.py:59
  328.1 0.8 add_convert_fusion
  329.0 2.9 gather_fusion
  332.0 0.2 gather.7
  332.2 0.5 broadcast.116
  332.7 0.7 reduce.5
  333.4 13.6 %all_to_all.6 = bf16[16,2,1152]{2,1,0:T(2,128)(2,1)S(1)} all-to-all(bf16[16,2,1152]{2,1,0:T(2,128)(2,1)S(1)} %reshape.169), channel_id=1, replica_groups=mesh['grp'=16,'mdl'=32] {'grp'}, dimensions={0} | all-to-all | bytes 147456 | tf_op jit(solution)/shard_map/all_to_all | solution.py:66
  347.0 0.4 reduce.1
  347.5 0.2 reshape.154
  347.7 0.8 copy.30
  348.6 0.2 dynamic-slice_reduce_fusion
  348.9 78.2 %all-gather.8.cloned.1.call-done = bf16[1152,1024]{0,1:T(8,128)(2,1)} async-done(((bf16[1152,32]{0,1:T(8,128)(2,1)}), bf16[1152,1024]{0,1:T(8,128)(2,1)}) %all-gather.8.cloned.1.call-update) | async-done | bytes 2359312 | tf_op jit(solution)/shard_map/all_gather | solution.py:67
  427.1 2.3 fusion.2
  429.5 3.5 fusion.8
  432.9 1.2 fusion.40
  434.2 5.5 fusion.41
  439.7 2.9 fusion.17
  442.6 1.3 convolution_convert_fusion.1
  443.9 219.4 %reduce-scatter.5.cloned.1.call-done = bf16[8,1024]{1,0:T(8,128)(2,1)} async-done(((bf16[256,1024]{1,0:T(8,128)(2,1)}), bf16[8,1024]{1,0:T(8,128)(2,1)}) %reduce-scatter.5.cloned.1.call-update) | async-done | bytes 16400 | tf_op jit(solution)/shard_map/reduce_scatter | solution.py:89
  (39 shorter events, 1.0 us)
Async XLA Ops:
  6.5 422.9 %copy-start = (bf16[2,1024,512]{2,1,0:T(8,128)(2,1)S(1)}, bf16[2,1024,512]{2,1,0:T(8,128)(2,1)}, u32[]{:S(2)}) copy-start(bf16[2,1024,512]{2,1,0:T(8,128)(2,1)} %param.14) | copy-start | bytes 6291460
  6.5 58.4 %all-gather.4.cloned.1.call-start = ((), (), s32[]{:S(2)}) async-start(), calls=%async_computation.3 | async-start | bytes 2228224 | tf_op jit(solution)/shard_map/all_gather | solution.py:50
  7.3 91.3 %all-gather.6.cloned.1.call-start = ((), (), s32[]{:S(2)}) async-start(), calls=%async_computation.4 | async-start | bytes 2228224 | tf_op jit(solution)/shard_map/all_gather | solution.py:56
  8.0 320.1 %reduce-scatter.3.cloned.1.call-start = ((), (), s32[]{:S(2)}) async-start(), calls=%async_computation.5 | async-start | bytes 1622016 | tf_op jit(solution)/shard_map/reduce_scatter | solution.py:59
  64.9 39.3 %copy-start.4 = (s32[6144]{0:T(1024)S(1)}, s32[6144]{0:T(1024)}, u32[]{:S(2)}) copy-start(s32[6144]{0:T(1024)} %param.17) | copy-start | bytes 73732
  104.1 224.0 %copy-start.3 = (bf16[384,32]{0,1:T(8,128)(2,1)S(1)}, bf16[384,32]{0,1:T(8,128)(2,1)}, u32[]{:S(2)}) copy-start(bf16[384,32]{0,1:T(8,128)(2,1)} %param.9) | copy-start | bytes 73732
  104.1 322.9 %all-gather.8.cloned.1.call-start = ((), (), s32[]{:S(2)}) async-start(), calls=%async_computation.6 | async-start | bytes 2433024 | tf_op jit(solution)/shard_map/all_gather | solution.py:67
  329.0 19.5 %copy-start.5 = (bf16[1024]{0:T(1024)(128)(2,1)S(1)}, bf16[1024]{0:T(1024)(128)(2,1)}, u32[]{:S(2)}) copy-start(bf16[1024]{0:T(1024)(128)(2,1)} %param.13) | copy-start | bytes 6148
  348.5 314.8 %reduce-scatter.5.cloned.1.call-start = ((), (), s32[]{:S(2)}) async-start(), calls=%async_computation.7 | async-start | bytes 540672 | tf_op jit(solution)/shard_map/reduce_scatter | solution.py:89
  427.1 2.4 copy-start.1
  432.9 1.2 copy-start.6
  439.7 3.0 copy-start.2
Sparse Core Ops, SparseCore 0:
  9.5 46.1 all-gather.3
  57.7 40.7 all-gather.5
  104.3 223.7 reduce-scatter.2
  348.6 78.4 all-gather.7
  444.0 219.2 reduce-scatter.4
where the time goes:
time: 670 us
  waiting for transfers between devices  555 us (83%)
  blocking collectives  69.5 us (10%)
  matrix products  18.7 us (3%)
  between operations  13.3 us (2%)
  local copies, waits for them, and re-layouts  7.41 us (1%)
    reduce_scatter x1, waiting for transfers between devices, local(): lax.psum_scatter(ffn_terms, 'mdl', scatter_dimension=1, tiled=True)  222 us
    reduce_scatter x1, waiting for transfers between devices, local(): lax.psum_scatter(jnp.dot(attended, attn_out, preferred_element_type=jnp.f...  219 us
    all_gather x1, waiting for transfers between devices, local(): lax.all_gather(arrived.reshape(groups * capacity, -1), 'mdl', axis=1, til...  78.2 us
    all_gather x1, blocking collectives, local(): full_rows = lax.all_gather(row_states, 'mdl', axis=1, tiled=True)  56 us
    all_gather x1, waiting for transfers between devices, local(): lax.all_gather(ffn_out, 'grp', axis=1, tiled=True)  33.6 us
    all_to_all x1, blocking collectives, local(): lax.all_to_all(outgoing, 'grp', split_axis=0, concat_axis=0, tiled=True)  13.6 us
  transfers between devices with their start and end apart: 5, of which 4 were waited for; matrix products, arithmetic and copies ran while one was open for 0% of the time, Pallas kernels for 0%

commit v1 on v0

--- a/solution.py
+++ b/solution.py
@@ -4,6 +4,22 @@
 from jax.sharding import PartitionSpec as P
 
 HEAD_DIM = 128
+
+
+def gather_around(x, axis, dim):
+    ways, here, step = (lax.axis_size(axis), lax.axis_index(axis), x.shape[dim])
+    shape = [n * ways if d == dim else n for d, n in enumerate(x.shape)]
+    full = lax.dynamic_update_slice_in_dim(jnp.zeros(shape, x.dtype), x, here * step, axis=dim)
+    going_up = going_down = x
+    for far in range(1, ways // 2 + 1):
+        going_up = lax.ppermute(going_up, axis, [(d, (d + 1) % ways) for d in range(ways)])
+        full = lax.dynamic_update_slice_in_dim(full, going_up, (here - far) % ways * step, axis=dim)
+        if 2 * far < ways:
+            going_down = lax.ppermute(going_down, axis, [(d, (d - 1) % ways) for d in range(ways)])
+            full = lax.dynamic_update_slice_in_dim(
+                full, going_down, (here + far) % ways * step, axis=dim
+            )
+    return full
 
 
 def rms_normalize(states, gain):
@@ -52,9 +68,7 @@
     )
     hidden = jnp.maximum(pre_active, 0.0).astype(jnp.bfloat16)
     ffn_terms = jnp.dot(
-        hidden,
-        lax.all_gather(ffn_out, "grp", axis=1, tiled=True),
-        preferred_element_type=jnp.float32,
+        hidden, gather_around(ffn_out, "grp", 1), preferred_element_type=jnp.float32
     )
     ffn_sum = lax.psum_scatter(ffn_terms, "mdl", scatter_dimension=1, tiled=True)
     enc_state = (row_states.astype(jnp.float32) + ffn_sum).astype(jnp.bfloat16)

time: 670 us -> 679 us (1.013)
  waiting for transfers between devices: 555 us -> 536 us
  starting transfers between devices: 0.16 us -> 14.8 us
  local copies, waits for them, and re-layouts: 7.41 us -> 19.9 us
    all_gather x1 -> x0, waiting for transfers between devices: 33.6 us -> none  [local(): lax.all_gather(ffn_out, 'grp', axis=1, tiled=True)]
    ppermute x0 -> x15, starting transfers between devices: none -> 14.5 us  [the longest x7 14.4 us: gather_around(): lax.ppermute(going_down, axis, [(d, (d - 1) % ways) for d in range(ways)])]
    ppermute x0 -> x15, waiting for transfers between devices: none -> 11.8 us  [the longest x8 11.3 us: gather_around(): lax.ppermute(going_up, axis, [(d, (d + 1) % ways) for d in range(ways)])]
    dynamic_update_slice x0 -> x16, local copies, waits for them, and re-layouts: none -> 10.6 us  [the longest x8 5.28 us: gather_around(): lax.dynamic_update_slice_in_dim(full, going_up, (here - far) % ways * ste...]
  transfers between devices with their start and end apart: 5 -> 19, of which waited for: 4 -> 13; matrix products, arithmetic and copies ran while one was open for 0% -> 2% of each run, Pallas kernels for 0% -> 0%
where the time goes in v1:
time: 679 us
  waiting for transfers between devices  536 us (79%)
  blocking collectives  69.6 us (10%)
  local copies, waits for them, and re-layouts  19.9 us (3%)
  matrix products  19.1 us (3%)
  starting transfers between devices  14.8 us (2%)
  between operations  13.7 us (2%)
    reduce_scatter x1, waiting for transfers between devices, local(): lax.psum_scatter(ffn_terms, 'mdl', scatter_dimension=1, tiled=True)  226 us
    reduce_scatter x1, waiting for transfers between devices, local(): lax.psum_scatter(jnp.dot(attended, attn_out, preferred_element_type=jnp.f...  220 us
    all_gather x1, waiting for transfers between devices, local(): lax.all_gather(arrived.reshape(groups * capacity, -1), 'mdl', axis=1, til...  78 us
    all_gather x1, blocking collectives, local(): full_rows = lax.all_gather(row_states, 'mdl', axis=1, tiled=True)  56 us
    ppermute x7, starting transfers between devices, gather_around(): lax.ppermute(going_down, axis, [(d, (d - 1) % ways) for d in range(ways)])  14.4 us
    all_to_all x1, blocking collectives, local(): lax.all_to_all(outgoing, 'grp', split_axis=0, concat_axis=0, tiled=True)  13.6 us
  transfers between devices with their start and end apart: 19, of which 13 were waited for; matrix products, arithmetic and copies ran while one was open for 2% of the time, Pallas kernels for 0%

profile of v1, /device:TPU:8, one launch (start us, length us, event | category | flops | bytes accessed | tf_op | source)
XLA Modules:
  0.0 678.8 jit_solution(4967779151182035948)
XLA Ops:
  6.5 0.7 all-gather.3.cloned.1.call-update
  7.3 1.7 collective-permute-start.1
  9.1 56.0 %all_gather.9 = bf16[384,1024]{0,1:T(8,128)(2,1)S(1)} all-gather(bf16[384,32]{0,1:T(8,128)(2,1)} %param.9), channel_id=1, replica_groups=mesh['grp'=16,'mdl'=32] {'mdl'}, dimensions={1}, use_global_device_ids=true | all-gather | bytes 811008 | tf_op jit(solution)/shard_map/all_gather | solution.py:62
  65.6 1.6 broadcast_in_dim.67
  67.9 1.7 collective-permute-start.3
  70.9 1.3 collective-permute-done.2
  72.3 2.0 collective-permute-start.5
  75.6 1.0 collective-permute-done.4
  76.8 1.9 collective-permute-start.7
  80.0 1.0 collective-permute-done.6
  81.2 1.9 collective-permute-start.9
  83.1 0.7 constant_dynamic-update-slice_fusion.8
  84.4 1.0 collective-permute-done.8
  85.6 2.2 collective-permute-start.11
  89.1 1.3 collective-permute-done.10
  90.4 3.0 collective-permute-start.13
  94.8 1.3 collective-permute-done.12
  97.4 4.3 collective-permute-done.14
  102.3 5.6 fusion.22
  109.8 226.2 %reduce-scatter.3.cloned.1.call-done = f32[384,32]{0,1:T(8,128)} async-done(((f32[384,1024]{0,1:T(8,128)}), f32[384,32]{0,1:T(8,128)}) %reduce-scatter.3.cloned.1.call-update) | async-done | bytes 49168 | tf_op jit(solution)/shard_map/reduce_scatter | solution.py:73
  336.0 0.8 add_convert_fusion
  336.9 2.9 gather_fusion
  341.3 13.6 %all_to_all.6 = bf16[16,2,1152]{2,1,0:T(2,128)(2,1)S(1)} all-to-all(bf16[16,2,1152]{2,1,0:T(2,128)(2,1)S(1)} %reshape.169), channel_id=1, replica_groups=mesh['grp'=16,'mdl'=32] {'grp'}, dimensions={0} | all-to-all | bytes 147456 | tf_op jit(solution)/shard_map/all_to_all | solution.py:80
  355.6 0.8 copy.30
  357.0 78.0 %all-gather.5.cloned.1.call-done = bf16[1152,1024]{0,1:T(8,128)(2,1)} async-done(((bf16[1152,32]{0,1:T(8,128)(2,1)}), bf16[1152,1024]{0,1:T(8,128)(2,1)}) %all-gather.5.cloned.1.call-update) | async-done | bytes 2359312 | tf_op jit(solution)/shard_map/all_gather | solution.py:81
  435.0 2.3 fusion.2
  437.4 3.5 fusion.8
  440.9 1.6 fusion.40
  442.5 5.5 fusion.41
  448.0 3.3 fusion.17
  451.3 1.3 convolution_convert_fusion.1
  452.6 219.6 %reduce-scatter.5.cloned.1.call-done = bf16[8,1024]{1,0:T(8,128)(2,1)} async-done(((bf16[256,1024]{1,0:T(8,128)(2,1)}), bf16[8,1024]{1,0:T(8,128)(2,1)}) %reduce-scatter.5.cloned.1.call-update) | async-done | bytes 16400 | tf_op jit(solution)/shard_map/reduce_scatter | solution.py:103
  (87 shorter events, 15.4 us)
Async XLA Ops:
  6.5 430.9 %copy-start = (bf16[2,1024,512]{2,1,0:T(8,128)(2,1)S(1)}, bf16[2,1024,512]{2,1,0:T(8,128)(2,1)}, u32[]{:S(2)}) copy-start(bf16[2,1024,512]{2,1,0:T(8,128)(2,1)} %param.14) | copy-start | bytes 6291460
  6.5 59.0 %copy-start.6 = (bf16[1024]{0:T(1024)(128)(2,1)S(1)}, bf16[1024]{0:T(1024)(128)(2,1)}, u32[]{:S(2)}) copy-start(bf16[1024]{0:T(1024)(128)(2,1)} %param.10) | copy-start | bytes 6148
  6.5 95.8 %all-gather.3.cloned.1.call-start = ((), (), s32[]{:S(2)}) async-start(), calls=%async_computation.3 | async-start | bytes 2228224 | tf_op jit(solution)/shard_map/all_gather | solution.py:66
  7.3 60.0 %copy-start.3 = (bf16[1024,64]{0,1:T(8,128)(2,1)S(1)}, bf16[1024,64]{0,1:T(8,128)(2,1)}, u32[]{:S(2)}) copy-start(bf16[1024,64]{0,1:T(8,128)(2,1)} %param.12) | copy-start | bytes 393220
  7.3 328.7 %reduce-scatter.3.cloned.1.call-start = ((), (), s32[]{:S(2)}) async-start(), calls=%async_computation.4 | async-start | bytes 1622016 | tf_op jit(solution)/shard_map/reduce_scatter | solution.py:73
  7.3 60.6 %collective-permute-start = (bf16[1024,64]{0,1:T(8,128)(2,1)}, bf16[1024,64]{0,1:T(8,128)(2,1)S(1)}, u32[]{:S(2)}, u32[]{:S(2)}) collective-permute-start(bf16[1024,64]{0,1:T(8,128)(2,1)} %param.12), channel_id=1, source_target_pairs={{0,32},{32,64},{64,96},{96,128},{128,160},{160,192},{192,224},{224... | collective-permute-start | bytes 393224 | tf_op jit(solution)/shard_map/ppermute | solution.py:15
  7.3 60.5 %collective-permute-start.1 = (bf16[1024,64]{0,1:T(8,128)(2,1)}, bf16[1024,64]{0,1:T(8,128)(2,1)S(1)}, u32[]{:S(2)}, u32[]{:S(2)}) collective-permute-start(bf16[1024,64]{0,1:T(8,128)(2,1)} %param.12), channel_id=1, source_target_pairs={{0,480},{32,0},{64,32},{96,64},{128,96},{160,128},{192,160},{224,1... | collective-permute-start | bytes 393224 | tf_op jit(solution)/shard_map/ppermute | solution.py:18
  67.9 4.4 collective-permute-start.2
  67.9 4.4 collective-permute-start.3
  72.3 4.4 collective-permute-start.4
  72.3 4.6 collective-permute-start.5
  76.7 4.4 collective-permute-start.6
  76.8 4.4 collective-permute-start.7
  81.1 4.4 collective-permute-start.8
  81.2 4.4 collective-permute-start.9
  85.5 5.0 collective-permute-start.10
  85.6 4.8 collective-permute-start.11
  90.4 5.6 collective-permute-start.12
  90.4 6.3 collective-permute-start.13
  96.1 5.6 collective-permute-start.14
  102.3 5.7 copy-start.5
  107.9 228.1 %copy-start.4 = (bf16[384,32]{0,1:T(8,128)(2,1)S(1)}, bf16[384,32]{0,1:T(8,128)(2,1)}, u32[]{:S(2)}) copy-start(bf16[384,32]{0,1:T(8,128)(2,1)} %param.9) | copy-start | bytes 73732
  108.0 327.1 %all-gather.5.cloned.1.call-start = ((), (), s32[]{:S(2)}) async-start(), calls=%async_computation.5 | async-start | bytes 2433024 | tf_op jit(solution)/shard_map/all_gather | solution.py:81
  336.9 19.7 %copy-start.7 = (bf16[1024]{0:T(1024)(128)(2,1)S(1)}, bf16[1024]{0:T(1024)(128)(2,1)}, u32[]{:S(2)}) copy-start(bf16[1024]{0:T(1024)(128)(2,1)} %param.13) | copy-start | bytes 6148
  356.4 315.8 %reduce-scatter.5.cloned.1.call-start = ((), (), s32[]{:S(2)}) async-start(), calls=%async_computation.6 | async-start | bytes 540672 | tf_op jit(solution)/shard_map/reduce_scatter | solution.py:103
  435.0 2.4 copy-start.1
  440.9 1.6 copy-start.8
  448.0 3.3 copy-start.2
Sparse Core Ops, SparseCore 0:
  9.5 45.9 all-gather.2
  108.1 227.8 reduce-scatter.2
  356.5 78.4 all-gather.4
  452.7 219.4 reduce-scatter.4
